TPU v7x, 32 devices: a whole 2x2x4 slice. The times are simulated.
32 devices in a mesh: groups: 2 (over y), seq: 4 (over z), tensor: 4 (over x, core).
Axes of the slice: x: 2, y: 2, z: 4, core: 2. Of those that a mesh axis runs over, the one named last changes fastest.
Arguments:
- video_query: bfloat16 [1024, 4096], P(('groups', 'seq'), 'tensor'), parts along dimension 0, may hold values from -21 to 21
- video_key: bfloat16 [1024, 4096], P(('groups', 'seq'), 'tensor'), parts along dimension 0, may hold values from -21 to 21
- video_value: bfloat16 [1024, 4096], P(('groups', 'seq'), 'tensor'), parts along dimension 0, may hold values from -6 to 6
- video_stream: bfloat16 [1024, 4096], P(('groups', 'seq'), 'tensor'), parts along dimension 0, may hold values from -6 to 6
- out_weight: bfloat16 [4096, 4096], P('tensor'), may hold values from -0.09375 to 0.09375
- cross_query: bfloat16 [1024, 2048], P(('groups', 'seq'), 'tensor'), parts along dimension 0, may hold values from -21 to 21
- audio_key: bfloat16 [128, 2048], P(('groups', 'seq'), 'tensor'), parts along dimension 0, may hold values from -21 to 21
- audio_value: bfloat16 [128, 2048], P(('groups', 'seq'), 'tensor'), parts along dimension 0, may hold values from -6 to 6
- audio_query: bfloat16 [128, 2048], P(('groups', 'seq'), 'tensor'), parts along dimension 0, may hold values from -21 to 21
- cross_key: bfloat16 [1024, 2048], P(('groups', 'seq'), 'tensor'), parts along dimension 0, may hold values from -21 to 21
- cross_value: bfloat16 [1024, 2048], P(('groups', 'seq'), 'tensor'), parts along dimension 0, may hold values from -6 to 6
Outputs:
- video_next: bfloat16 [1024, 4096], P(('groups', 'seq'), 'tensor'), parts along dimension 0
- video_cross: bfloat16 [1024, 2048], P(('groups', 'seq'), 'tensor'), parts along dimension 0
- audio_cross: bfloat16 [128, 2048], P(('groups', 'seq'), 'tensor'), parts along dimension 0
There are 2 independent parts, one for each index of `groups`. A program takes and returns all parts, laid end to end along the dimension named above; an argument that names none is the same for every part. Nothing has to cross between parts.
All inputs are finite; a program needn't handle non-finite values.
Results may differ from a plain program's by a relative error of at most 0.012.
Values may be sent and summed in bfloat16 or wider, within the bound.
A program may use at most 64 MiB of HBM per device.

v0:
```python
import functools
import math

import jax
import jax.numpy as jnp
from jax import lax
from jax.experimental import pallas as pl
from jax.experimental.pallas import tpu as pltpu
from jax.sharding import PartitionSpec as P

HD = 128


def blank_state(query_rows, head_count):
    return (
        jnp.full((head_count, query_rows), -1e30, jnp.float32),
        jnp.zeros((head_count, query_rows), jnp.float32),
        jnp.zeros((head_count, query_rows, HD), jnp.float32),
    )


def absorb(carried, queries, keyset, values, head_count):
    running, row_sum, numerator = carried
    query_rows = queries.shape[0]
    key_rows = keyset.shape[0]
    factor = 1.0 / math.sqrt(HD)
    query_heads = queries.reshape(query_rows, head_count, HD)
    for offset in range(0, key_rows, 1024):
        width_keys = min(1024, key_rows - offset)
        key_block = keyset[offset : offset + width_keys].reshape(width_keys, head_count, HD)
        value_block = values[offset : offset + width_keys].reshape(width_keys, head_count, HD)
        scores = (
            jnp.einsum("qhd,khd->hqk", query_heads, key_block, preferred_element_type=jnp.float32)
            * factor
        )
        highest = jnp.maximum(running, jnp.max(scores, axis=2))
        raised = jnp.exp(scores - highest[:, :, None])
        shrink = jnp.exp(running - highest)
        row_sum = row_sum * shrink + jnp.sum(raised, axis=2)
        numerator = numerator * shrink[:, :, None] + jnp.einsum(
            "hqk,khd->hqd",
            raised.astype(jnp.bfloat16),
            value_block,
            preferred_element_type=jnp.float32,
        )
        running = highest
    return (running, row_sum, numerator)


def finish(carried, head_count):
    running, row_sum, numerator = carried
    result = numerator / row_sum[:, :, None]
    return result.transpose(1, 0, 2).reshape(result.shape[1], head_count * HD).astype(jnp.bfloat16)


def local(
    video_query,
    video_key,
    video_value,
    video_stream,
    out_weight,
    cross_query,
    audio_key,
    audio_value,
    audio_query,
    cross_key,
    cross_value,
):
    local_heads = video_query.shape[1] // HD
    query_rows = video_query.shape[0]
    pieces = (
        lax.all_gather(video_key, "seq", axis=0, tiled=True),
        lax.all_gather(video_value, "seq", axis=0, tiled=True),
    )
    carried_video = absorb(
        blank_state(query_rows, local_heads), video_query, pieces[0], pieces[1], local_heads
    )
    attended = finish(carried_video, local_heads)
    projected = jnp.dot(attended, out_weight, preferred_element_type=jnp.float32)
    summed = lax.psum_scatter(
        projected.astype(jnp.bfloat16), "tensor", scatter_dimension=1, tiled=True
    ).astype(jnp.float32)
    video_next = (video_stream.astype(jnp.float32) + summed).astype(jnp.bfloat16)
    cross_heads = cross_query.shape[1] // HD
    every_key, every_value = (
        lax.all_gather(audio_key, "seq", axis=0, tiled=True),
        lax.all_gather(audio_value, "seq", axis=0, tiled=True),
    )
    carried_audio = absorb(
        blank_state(cross_query.shape[0], cross_heads),
        cross_query,
        every_key,
        every_value,
        cross_heads,
    )
    video_cross = finish(carried_audio, cross_heads)
    pieces = (
        lax.all_gather(cross_key, "seq", axis=0, tiled=True),
        lax.all_gather(cross_value, "seq", axis=0, tiled=True),
    )
    carried_cross = absorb(
        blank_state(audio_query.shape[0], cross_heads),
        audio_query,
        pieces[0],
        pieces[1],
        cross_heads,
    )
    audio_cross = finish(carried_cross, cross_heads)
    return (video_next, video_cross, audio_cross)


MESH = pl.DeviceIdType.MESH
NT = (((1,), (1,)), ((), ()))
WIDE = 512
FIRST = 4


def softmax_parts(queries, keyset, values):
    scores = lax.dot_general(queries, keyset, NT, preferred_element_type=jnp.float32) * (
        1.0 / math.sqrt(HD)
    )
    highest = jnp.max(scores, axis=1, keepdims=True)
    raised = jnp.exp(scores - highest)
    row_sum = jnp.sum(raised, axis=1, keepdims=True)
    numerator = jnp.dot(raised.astype(jnp.bfloat16), values, preferred_element_type=jnp.float32)
    return highest, row_sum, numerator


def block_kernel(
    seq,
    tensor,
    vq,
    vk,
    vv,
    vs,
    weight,
    cq,
    ak,
    av,
    aq,
    ck,
    cv,
    next_ref,
    vcross_ref,
    across_ref,
    qkv,
    heads_out,
    gathered,
    audio,
    partial,
    stats,
    partial_in,
    stats_in,
    cq_v,
    ck_v,
    cv_v,
    stream_v,
    weight_v,
    kept,
    pair_out,
    pair_in,
    far_out,
    far_in,
    kv_send,
    kv_recv,
    q_send,
    q_recv,
    own_sem,
    out_send,
    out_recv,
    audio_send,
    audio_recv,
    audio_own,
    part_send,
    part_recv,
    stat_send,
    stat_recv,
    load_sem,
    weight_sem,
    pair_send,
    pair_recv,
    far_send,
    far_recv,
):
    rows = vq.shape[0]
    share = vq.shape[1] // HD // seq
    cross_heads = cq.shape[1] // HD
    audio_rows = aq.shape[0]
    chips = tensor // 2
    width = next_ref.shape[1]
    pieces = width // WIDE
    cuts = row_cuts(rows)
    me = lax.axis_index("seq")
    place = lax.axis_index("tensor")
    core = lax.rem(place, 2)
    chip = place // 2
    sibling = chip * 2 + (1 - core)
    peers = [lax.rem(me + d, seq) for d in range(1, seq)]
    far_chips = [lax.rem(chip + d, chips) for d in range(chips)]

    my_rows = pl.ds(pl.multiple_of(me * rows, rows), rows)
    my_audio = pl.ds(pl.multiple_of(me * audio_rows, audio_rows), audio_rows)

    def head_cols(owner, h):
        return pl.ds(pl.multiple_of((owner * share + h) * HD, HD), HD)

    local_copies = []
    for h in range(share):
        for kind, ref in enumerate((vk, vv, vq)):
            copy = pltpu.make_async_copy(
                ref.at[:, head_cols(me, h)], qkv.at[kind, h, my_rows], own_sem.at[kind, h]
            )
            copy.start()
            local_copies.append(copy)
    audio_copies = []
    for kind, ref in enumerate((ak, av, aq)):
        copy = pltpu.make_async_copy(ref, audio.at[kind, my_audio], audio_own.at[kind])
        copy.start()
        audio_copies.append(copy)
    loads = []
    for i, (ref, dst) in enumerate(((cq, cq_v), (ck, ck_v), (cv, cv_v), (vs, stream_v))):
        copy = pltpu.make_async_copy(ref, dst, load_sem.at[i])
        copy.start()
        loads.append(copy)

    barrier = pltpu.get_barrier_semaphore()
    for p in peers:
        pl.semaphore_signal(barrier, inc=1, device_id={"seq": p}, device_id_type=MESH)
    pl.semaphore_signal(barrier, inc=1, device_id={"tensor": sibling}, device_id_type=MESH)
    for d in range(1, chips):
        pl.semaphore_signal(
            barrier, inc=1, device_id={"tensor": far_chips[d] * 2 + core}, device_id_type=MESH
        )
    pl.semaphore_wait(barrier, seq - 1 + chips)

    sends = []

    def to_seq(src, dst, send_sem, recv_sem, p):
        return pltpu.make_async_remote_copy(
            src_ref=src,
            dst_ref=dst,
            send_sem=send_sem,
            recv_sem=recv_sem,
            device_id={"seq": p},
            device_id_type=MESH,
        )

    def launch(copy):
        copy.start()
        sends.append(copy)

    def cut_of(p, r):
        start, size = cuts[r]
        return pl.ds(pl.multiple_of(p * rows + start, 16), size)

    def send_queries(r):
        start, size = cuts[r]
        for h in range(share):
            for p in peers:
                launch(
                    to_seq(
                        vq.at[pl.ds(start, size), head_cols(p, h)],
                        qkv.at[2, h, cut_of(me, r)],
                        q_send.at[r, h, p],
                        q_recv.at[r, h, me],
                        p,
                    )
                )

    def rows_of(p):
        return pl.ds(pl.multiple_of(p * rows, rows), rows)

    def audio_rows_of(p):
        return pl.ds(pl.multiple_of(p * audio_rows, audio_rows), audio_rows)

    def audio_hop(step, way):
        shard = lax.rem(me - way * step + seq, seq)
        here = audio_rows_of(shard)
        return to_seq(
            audio.at[:, here],
            audio.at[:, here],
            audio_send.at[step, (way + 1) // 2],
            audio_recv.at[shard],
            lax.rem(me + way + seq, seq),
        )

    def on_line(step, way):
        source, target = me - way * step, me + way
        return (source >= 0) & (source < seq) & (target >= 0) & (target < seq)

    def pass_audio(step):
        for way in (1, -1):

            @pl.when(on_line(step, way))
            def _():
                copy = audio_hop(step, way)
                if step:
                    copy.wait_recv()
                copy.start()

    def end_audio():
        for step in range(1, seq):
            for way in (1, -1):
                source, target = me - way * step, me + way
                last = (target < 0) | (target >= seq)

                @pl.when((source >= 0) & (source < seq) & last)
                def _():
                    audio_hop(step, way).wait_recv()

    for copy in audio_copies:
        copy.wait()
    pass_audio(0)
    for h in range(share):
        for kind, ref in enumerate((vk, vv)):
            for p in peers:
                launch(
                    to_seq(
                        ref.at[:, head_cols(p, h)],
                        qkv.at[kind, h, my_rows],
                        kv_send.at[kind, h, p],
                        kv_recv.at[kind, h, me],
                        p,
                    )
                )
    pass_audio(1)
    send_queries(0)
    for r in range(1, len(cuts)):
        send_queries(r)

    weight_copy = pltpu.make_async_copy(weight, weight_v, weight_sem)
    weight_copy.start()

    def wait_from(src, dst, send_sem, recv_sem, p):
        to_seq(src, dst, send_sem, recv_sem, p).wait_recv()

    def wait_keys():
        for copy in local_copies:
            copy.wait()
        for h in range(share):
            for kind, ref in enumerate((vk, vv)):
                for p in peers:
                    wait_from(
                        ref.at[:, head_cols(p, h)],
                        qkv.at[kind, h, rows_of(p)],
                        kv_send.at[kind, h, p],
                        kv_recv.at[kind, h, p],
                        p,
                    )

    def attend_rows(r):
        start, size = cuts[r]
        here = pl.ds(start, size)
        for h in range(share):
            keyset, values = qkv[0, h], qkv[1, h]
            for p in peers + [me]:
                if p is not me:
                    wait_from(
                        vq.at[here, head_cols(p, h)],
                        qkv.at[2, h, cut_of(p, r)],
                        q_send.at[r, h, p],
                        q_recv.at[r, h, p],
                        p,
                    )
                _, row_sum, numerator = softmax_parts(qkv[2, h, cut_of(p, r)], keyset, values)
                result = (numerator / row_sum).astype(jnp.bfloat16)
                if p is me:
                    gathered[h, me, here] = result
                else:
                    heads_out[h, p, here] = result
                    launch(
                        to_seq(
                            heads_out.at[h, p, here],
                            gathered.at[h, me, here],
                            out_send.at[r, h, p],
                            out_recv.at[r, h, me],
                            p,
                        )
                    )

    def cross_parts():
        for i in range(3):
            loads[i].wait()
        end_audio()
        lane = lax.broadcasted_iota(jnp.int32, (seq * audio_rows, HD), 1)
        held = jnp.zeros((seq * audio_rows, HD), jnp.float32)
        for c in range(cross_heads):
            cols = slice(c * HD, (c + 1) * HD)
            highest, row_sum, numerator = softmax_parts(audio[2, :, cols], ck_v[:, cols], cv_v[:, cols])
            held = jnp.where(lane == c, highest, held)
            held = jnp.where(lane == cross_heads + c, row_sum, held)
            partial[:, cols] = numerator.astype(jnp.bfloat16)
        stats[...] = held
        for p in peers:
            for src, dst, s_sem, r_sem in (
                (partial, partial_in, part_send, part_recv),
                (stats, stats_in, stat_send, stat_recv),
            ):
                copy = pltpu.make_async_remote_copy(
                    src_ref=src.at[audio_rows_of(p)],
                    dst_ref=dst.at[me],
                    send_sem=s_sem.at[p],
                    recv_sem=r_sem.at[me],
                    device_id={"seq": p},
                    device_id_type=MESH,
                )
                copy.start()
                sends.append(copy)
        for c in range(cross_heads):
            cols = slice(c * HD, (c + 1) * HD)
            _, row_sum, numerator = softmax_parts(cq_v[:, cols], audio[0, :, cols], audio[1, :, cols])
            vcross_ref[:, cols] = (numerator / row_sum).astype(jnp.bfloat16)

    def cross_finish():
        for p in peers:
            wait_from(partial.at[audio_rows_of(p)], partial_in.at[p], part_send.at[p], part_recv.at[p], p)
            wait_from(stats.at[audio_rows_of(p)], stats_in.at[p], stat_send.at[p], stat_recv.at[p], p)
        held = [stats[my_audio, :]] + [stats_in[p] for p in peers]
        for c in range(cross_heads):
            cols = slice(c * HD, (c + 1) * HD)
            parts = [partial[my_audio, cols]] + [partial_in[p, :, cols] for p in peers]
            tops = [s[:, c : c + 1] for s in held]
            sums = [s[:, cross_heads + c : cross_heads + c + 1] for s in held]
            highest = functools.reduce(jnp.maximum, tops)
            factors = [jnp.exp(t - highest) for t in tops]
            row_sum = sum(f * s for f, s in zip(factors, sums))
            numerator = sum(f * n.astype(jnp.float32) for f, n in zip(factors, parts))
            across_ref[:, cols] = (numerator / row_sum).astype(jnp.bfloat16)

    def wait_heads(r):
        here = pl.ds(*cuts[r])
        for h in range(share):
            for p in peers:
                wait_from(
                    heads_out.at[h, p, here],
                    gathered.at[h, p, here],
                    out_send.at[r, h, p],
                    out_recv.at[r, h, p],
                    p,
                )
        return jnp.concatenate(
            [gathered[h, p, here] for p in range(seq) for h in range(share)], axis=1
        )

    def product(attended, d, side, j):
        target = far_chips[d] * 2 + (core if side else 1 - core)
        cols = pl.ds(pl.multiple_of(target * width + j * WIDE, WIDE), WIDE)
        return jnp.dot(attended, weight_v[:, cols], preferred_element_type=jnp.float32)

    def pair_copy(r, d, j):
        here = pl.ds(*cuts[r])
        return pltpu.make_async_remote_copy(
            src_ref=pair_out.at[d, j, here],
            dst_ref=pair_in.at[d, j, here],
            send_sem=pair_send.at[r, d, j],
            recv_sem=pair_recv.at[r, d, j],
            device_id={"tensor": sibling},
            device_id_type=MESH,
        )

    def far_copy(r, d, j):
        here = pl.ds(*cuts[r])
        return pltpu.make_async_remote_copy(
            src_ref=far_out.at[d - 1, j, here],
            dst_ref=far_in.at[d - 1, j, here],
            send_sem=far_send.at[r, d - 1, j],
            recv_sem=far_recv.at[r, d - 1, j],
            device_id={"tensor": far_chips[d] * 2 + core},
            device_id_type=MESH,
        )

    def share_rows(r):
        here = pl.ds(*cuts[r])
        attended = wait_heads(r)
        if r == 0:
            weight_copy.wait()
        steps = [(d, j) for d in range(1, chips) for j in range(pieces)]
        for d, j in steps:
            pair_out[d, j, here] = product(attended, d, 0, j).astype(jnp.bfloat16)
            launch(pair_copy(r, d, j))
        for d, j in steps:
            mine = product(attended, d, 1, j)
            pair_copy(r, d, j).wait_recv()
            far_out[d - 1, j, here] = (mine + pair_in[d, j, here].astype(jnp.float32)).astype(
                jnp.bfloat16
            )
            launch(far_copy(r, d, j))
        for j in range(pieces):
            pair_out[0, j, here] = product(attended, 0, 0, j).astype(jnp.bfloat16)
            launch(pair_copy(r, 0, j))
        for j in range(pieces):
            block = slice(j * WIDE, (j + 1) * WIDE)
            kept[here, block] = product(attended, 0, 1, j) + stream_v[here, block].astype(jnp.float32)

    def close_rows(r):
        here = pl.ds(*cuts[r])
        for j in range(pieces):
            block = slice(j * WIDE, (j + 1) * WIDE)
            pair_copy(r, 0, j).wait_recv()
            value = kept[here, block] + pair_in[0, j, here].astype(jnp.float32)
            for d in range(1, chips):
                far_copy(r, d, j).wait_recv()
                value = value + far_in[d - 1, j, here].astype(jnp.float32)
            next_ref[here, block] = value.astype(jnp.bfloat16)

    wait_keys()
    for step in range(2, seq - 1):
        pass_audio(step)
    for r in range(len(cuts)):
        attend_rows(r)
    cross_parts()
    loads[3].wait()
    for r in range(len(cuts)):
        share_rows(r)
    cross_finish()
    for r in range(len(cuts)):
        close_rows(r)
    for copy in sends:
        copy.wait_send()
    for step in range(seq - 1):
        for way in (1, -1):

            @pl.when(on_line(step, way))
            def _():
                audio_hop(step, way).wait_send()


def row_cuts(rows):
    first = max(rows * FIRST // 4 // 16 * 16, 16)
    return [(0, first), (first, rows - first)] if first < rows else [(0, rows)]


def write_out(*refs):
    half = len(refs) // 2
    for src, dst in zip(refs[:half], refs[half:]):
        dst[...] = src[...]


def fused(seq, tensor, *operands):
    vq, vk, vv, vs, weight, cq, ak, av, aq, ck, cv = operands
    rows, features = vq.shape
    share = features // HD // seq
    audio_rows, cross_width = aq.shape
    chips = tensor // 2
    width = weight.shape[1] // tensor
    pieces = width // WIDE
    groups = len(row_cuts(rows))
    bf16, f32, dma = jnp.bfloat16, jnp.float32, pltpu.SemaphoreType.DMA
    shapes = tuple(jax.ShapeDtypeStruct(x.shape, bf16) for x in (vs, cq, aq))
    whole = pl.BlockSpec(memory_space=pltpu.VMEM)
    results = pl.pallas_call(
        functools.partial(block_kernel, seq, tensor),
        out_shape=tuple(pltpu.VMEM(x.shape, bf16) for x in (vs, cq, aq)),
        in_specs=[pl.BlockSpec(memory_space=pltpu.HBM)] * 11,
        out_specs=(whole,) * 3,
        scratch_shapes=[
            pltpu.VMEM((3, share, seq * rows, HD), bf16),
            pltpu.VMEM((share, seq, rows, HD), bf16),
            pltpu.VMEM((share, seq, rows, HD), bf16),
            pltpu.VMEM((3, seq * audio_rows, cross_width), bf16),
            pltpu.VMEM((seq * audio_rows, cross_width), bf16),
            pltpu.VMEM((seq * audio_rows, HD), f32),
            pltpu.VMEM((seq, audio_rows, cross_width), bf16),
            pltpu.VMEM((seq, audio_rows, HD), f32),
            pltpu.VMEM(cq.shape, bf16),
            pltpu.VMEM(ck.shape, bf16),
            pltpu.VMEM(cv.shape, bf16),
            pltpu.VMEM(vs.shape, bf16),
            pltpu.VMEM(weight.shape, bf16),
            pltpu.VMEM(vs.shape, f32),
            pltpu.VMEM((chips, pieces, rows, WIDE), bf16),
            pltpu.VMEM((chips, pieces, rows, WIDE), bf16),
            pltpu.VMEM((max(chips - 1, 1), pieces, rows, WIDE), bf16),
            pltpu.VMEM((max(chips - 1, 1), pieces, rows, WIDE), bf16),
            dma((2, share, seq)),
            dma((2, share, seq)),
            dma((groups, share, seq)),
            dma((groups, share, seq)),
            dma((3, share)),
            dma((groups, share, seq)),
            dma((groups, share, seq)),
            dma((seq, 2)),
            dma((seq,)),
            dma((3,)),
            dma((seq,)),
            dma((seq,)),
            dma((seq,)),
            dma((seq,)),
            dma((4,)),
            dma(()),
            dma((groups, chips, pieces)),
            dma((groups, chips, pieces)),
            dma((groups, max(chips - 1, 1), pieces)),
            dma((groups, max(chips - 1, 1), pieces)),
        ],
        compiler_params=pltpu.CompilerParams(
            collective_id=0, has_side_effects=True, vmem_limit_bytes=60000000
        ),
    )(*operands)
    return pl.pallas_call(
        write_out,
        out_shape=shapes,
        in_specs=[whole] * 3,
        out_specs=(whole,) * 3,
        compiler_params=pltpu.CompilerParams(vmem_limit_bytes=8 * 2**20),
    )(*results)


def fits(mesh, operands):
    seq, tensor = mesh.shape["seq"], mesh.shape["tensor"]
    vq, weight, cq, aq = operands[0], operands[4], operands[5], operands[8]
    return (
        seq > 1
        and (vq.shape[1] // HD) % seq == 0
        and tensor % 2 == 0
        and (weight.shape[1] // tensor) % WIDE == 0
        and aq.shape[0] % 16 == 0
        and vq.shape[0] % 16 == 0
        and 2 * (cq.shape[1] // HD) <= HD
        and weight.size * 2 <= 10 * 2**20
        and vq.shape[0] <= 128
        and seq <= 8
    )


def solution(mesh):
    def step(*operands):
        if fits(mesh, operands):
            return fused(mesh.shape["seq"], mesh.shape["tensor"], *operands)
        return local(*operands)

    in_specs = (
        P(("groups", "seq"), "tensor"),
        P(("groups", "seq"), "tensor"),
        P(("groups", "seq"), "tensor"),
        P(("groups", "seq"), "tensor"),
        P("tensor", None),
        P(("groups", "seq"), "tensor"),
        P(("groups", "seq"), "tensor"),
        P(("groups", "seq"), "tensor"),
        P(("groups", "seq"), "tensor"),
        P(("groups", "seq"), "tensor"),
        P(("groups", "seq"), "tensor"),
    )
    out_specs = (
        P(("groups", "seq"), "tensor"),
        P(("groups", "seq"), "tensor"),
        P(("groups", "seq"), "tensor"),
    )
    return jax.shard_map(step, mesh=mesh, in_specs=in_specs, out_specs=out_specs, check_vma=False)
```

profile of v0, /device:TPU:0, one launch (start us, length us, event | category | flops | bytes accessed | tf_op | source)
XLA Modules:
  0.0 43.4 jit_solution(14397748378109471345)
XLA Ops:
  0.6 42.0 %shard_map.130 = (bf16[128,1024]{1,0:T(8,128)(2,1)S(1)}, bf16[128,512]{1,0:T(8,128)(2,1)S(1)}, bf16[16,512]{1,0:T(8,128)(2,1)S(1)}) custom-call(bf16[128,1024]{1,0:T(8,128)(2,1)} %vq.1, bf16[128,1024]{1,0:T(8,128)(2,1)} %vk.1, bf16[128,1024]{1,0:T(8,128)(2,1)} %vv.1, bf16[128,1024]{1,0:T(8,128)(2,1)} %vs.1, bf16[1024,4096]{1,0:T(8,128)(2,1)} %weight.1, ...), custom_call_target="tpu_custom_call" | custom-call | tf_op jit(solution)/shard_map/pallas_call | solution.py:551
  42.6 0.8 %shard_map.131 = (bf16[128,1024]{1,0:T(8,128)(2,1)}, bf16[128,512]{1,0:T(8,128)(2,1)}, bf16[16,512]{1,0:T(8,128)(2,1)}) custom-call(bf16[128,1024]{1,0:T(8,128)(2,1)S(1)} %get-tuple-element.6.refs_0_, bf16[128,512]{1,0:T(8,128)(2,1)S(1)} %get-tuple-element.7.refs_1_, bf16[16,512]{1,0:T(8,128)(2,1)S(1)} %get-tuple-element.8.refs_2_), custom_call_target="tpu_custom_call" | custom-call | tf_op jit(solution)/shard_map/pallas_call | solution.py:600
where the time goes:
time: 43.6 us; the launch traced here: 43.4 us
  Pallas kernels  42.8 us (98%)
  between operations  0.64 us (1%)
    pallas_call x1, Pallas kernels, fused(): pl.pallas_call(functools.partial(block_kernel, seq, tensor), out_shape=tu...  42 us

commit v1 on v0

v1 whole, which is shorter than its diff:
```python
import functools
import math

import jax
import jax.numpy as jnp
from jax import lax
from jax.experimental import pallas as pl
from jax.experimental.pallas import tpu as pltpu
from jax.sharding import PartitionSpec as P

HD = 128


def blank_state(query_rows, head_count):
    return (
        jnp.full((head_count, query_rows), -1e30, jnp.float32),
        jnp.zeros((head_count, query_rows), jnp.float32),
        jnp.zeros((head_count, query_rows, HD), jnp.float32),
    )


def absorb(carried, queries, keyset, values, head_count):
    running, row_sum, numerator = carried
    query_rows = queries.shape[0]
    key_rows = keyset.shape[0]
    factor = 1.0 / math.sqrt(HD)
    query_heads = queries.reshape(query_rows, head_count, HD)
    for offset in range(0, key_rows, 1024):
        width_keys = min(1024, key_rows - offset)
        key_block = keyset[offset : offset + width_keys].reshape(width_keys, head_count, HD)
        value_block = values[offset : offset + width_keys].reshape(width_keys, head_count, HD)
        scores = (
            jnp.einsum("qhd,khd->hqk", query_heads, key_block, preferred_element_type=jnp.float32)
            * factor
        )
        highest = jnp.maximum(running, jnp.max(scores, axis=2))
        raised = jnp.exp(scores - highest[:, :, None])
        shrink = jnp.exp(running - highest)
        row_sum = row_sum * shrink + jnp.sum(raised, axis=2)
        numerator = numerator * shrink[:, :, None] + jnp.einsum(
            "hqk,khd->hqd",
            raised.astype(jnp.bfloat16),
            value_block,
            preferred_element_type=jnp.float32,
        )
        running = highest
    return (running, row_sum, numerator)


def finish(carried, head_count):
    running, row_sum, numerator = carried
    result = numerator / row_sum[:, :, None]
    return result.transpose(1, 0, 2).reshape(result.shape[1], head_count * HD).astype(jnp.bfloat16)


def local(
    video_query,
    video_key,
    video_value,
    video_stream,
    out_weight,
    cross_query,
    audio_key,
    audio_value,
    audio_query,
    cross_key,
    cross_value,
):
    local_heads = video_query.shape[1] // HD
    query_rows = video_query.shape[0]
    pieces = (
        lax.all_gather(video_key, "seq", axis=0, tiled=True),
        lax.all_gather(video_value, "seq", axis=0, tiled=True),
    )
    carried_video = absorb(
        blank_state(query_rows, local_heads), video_query, pieces[0], pieces[1], local_heads
    )
    attended = finish(carried_video, local_heads)
    projected = jnp.dot(attended, out_weight, preferred_element_type=jnp.float32)
    summed = lax.psum_scatter(
        projected.astype(jnp.bfloat16), "tensor", scatter_dimension=1, tiled=True
    ).astype(jnp.float32)
    video_next = (video_stream.astype(jnp.float32) + summed).astype(jnp.bfloat16)
    cross_heads = cross_query.shape[1] // HD
    every_key, every_value = (
        lax.all_gather(audio_key, "seq", axis=0, tiled=True),
        lax.all_gather(audio_value, "seq", axis=0, tiled=True),
    )
    carried_audio = absorb(
        blank_state(cross_query.shape[0], cross_heads),
        cross_query,
        every_key,
        every_value,
        cross_heads,
    )
    video_cross = finish(carried_audio, cross_heads)
    pieces = (
        lax.all_gather(cross_key, "seq", axis=0, tiled=True),
        lax.all_gather(cross_value, "seq", axis=0, tiled=True),
    )
    carried_cross = absorb(
        blank_state(audio_query.shape[0], cross_heads),
        audio_query,
        pieces[0],
        pieces[1],
        cross_heads,
    )
    audio_cross = finish(carried_cross, cross_heads)
    return (video_next, video_cross, audio_cross)


MESH = pl.DeviceIdType.MESH
NT = (((1,), (1,)), ((), ()))
WIDE = 512
SHARES = (3, 3, 2)


def softmax_parts(queries, keyset, values):
    scores = lax.dot_general(queries, keyset, NT, preferred_element_type=jnp.float32) * (
        1.0 / math.sqrt(HD)
    )
    highest = jnp.max(scores, axis=1, keepdims=True)
    raised = jnp.exp(scores - highest)
    row_sum = jnp.sum(raised, axis=1, keepdims=True)
    numerator = jnp.dot(raised.astype(jnp.bfloat16), values, preferred_element_type=jnp.float32)
    return highest, row_sum, numerator


def row_cuts(rows):
    tiles, whole = rows // 16, sum(SHARES)
    marks = sorted({tiles * sum(SHARES[: i + 1]) // whole for i in range(len(SHARES))} | {0})
    return [(16 * a, 16 * (b - a)) for a, b in zip(marks, marks[1:])]


def by_distance(me, seq):
    right = (me < seq - 1 - me).astype(jnp.int32)
    toward = 2 * right - 1
    short = right * me + (1 - right) * (seq - 1 - me)
    order = []
    for i in range(seq - 1):
        both = (i < 2 * short).astype(jnp.int32)
        near = (i // 2 + 1) * (1 if i % 2 == 0 else -1)
        order.append(me + toward * (both * near + (1 - both) * (i - short + 1)))
    return order


def block_kernel(
    seq,
    tensor,
    vq,
    vk,
    vv,
    vs,
    weight,
    cq,
    ak,
    av,
    aq,
    ck,
    cv,
    next_ref,
    vcross_ref,
    across_ref,
    kv,
    q_all,
    heads_out,
    gathered,
    audio,
    partial,
    stats,
    partial_in,
    stats_in,
    cross_v,
    stream_v,
    weight_v,
    kept,
    mine,
    pair_out,
    pair_in,
    far_out,
    far_in,
    token,
    kv_send,
    kv_recv,
    q_send,
    q_recv,
    own_kv,
    own_q,
    out_send,
    out_recv,
    audio_send,
    audio_recv,
    audio_own,
    part_send,
    part_recv,
    stat_send,
    stat_recv,
    cross_sem,
    stream_sem,
    weight_sem,
    pair_send,
    pair_recv,
    home_recv,
    far_send,
    far_recv,
):
    rows = vq.shape[0]
    span = vq.shape[1] // seq
    share = span // HD
    cross_heads = cq.shape[1] // HD
    audio_rows = aq.shape[0]
    chips = tensor // 2
    width = next_ref.shape[1]
    pieces = width // WIDE
    cuts = row_cuts(rows)
    groups = len(cuts)
    me = lax.axis_index("seq")
    place = lax.axis_index("tensor")
    core = lax.rem(place, 2)
    chip = place // 2
    sibling = chip * 2 + (1 - core)
    peers = by_distance(me, seq)
    far_chips = [lax.rem(chip + d, chips) for d in range(chips)]

    def rows_of(p):
        return pl.ds(pl.multiple_of(p * rows, rows), rows)

    def audio_rows_of(p):
        return pl.ds(pl.multiple_of(p * audio_rows, audio_rows), audio_rows)

    def cols_of(p):
        return pl.ds(pl.multiple_of(p * span, span), span)

    def slot(p, r):
        start, size = cuts[r]
        return pl.ds(pl.multiple_of(seq * start + p * size, 16), size)

    for kind, ref in enumerate((vk, vv)):
        pltpu.make_async_copy(ref.at[:, cols_of(me)], kv.at[kind, rows_of(me)], own_kv).start()
    for r in range(groups):
        pltpu.make_async_copy(vq.at[pl.ds(*cuts[r]), cols_of(me)], q_all.at[slot(me, r)], own_q).start()
    for kind, ref in enumerate((ak, av, aq)):
        pltpu.make_async_copy(ref, audio.at[kind, audio_rows_of(me)], audio_own).start()
    for kind, ref in enumerate((cq, ck, cv)):
        pltpu.make_async_copy(ref, cross_v.at[kind], cross_sem).start()
    stream_copy = pltpu.make_async_copy(vs, stream_v, stream_sem)
    stream_copy.start()

    def local_done(ref, sem):
        pltpu.make_async_copy(ref, ref, sem).wait()

    barrier = pltpu.get_barrier_semaphore()
    for way in (1, -1):

        @pl.when((me + way >= 0) & (me + way < seq))
        def _():
            pl.semaphore_signal(barrier, inc=1, device_id={"seq": me + way}, device_id_type=MESH)

    pl.semaphore_signal(barrier, inc=1, device_id={"tensor": sibling}, device_id_type=MESH)
    for d in range(1, chips):
        pl.semaphore_signal(
            barrier, inc=1, device_id={"tensor": far_chips[d] * 2 + core}, device_id_type=MESH
        )
    inner = ((me > 0) & (me < seq - 1)).astype(jnp.int32)
    with jax.named_scope("barrier"):
        pl.semaphore_wait(barrier, chips + 1 + inner)

    def to_seq(src, dst, send_sem, recv_sem, p):
        return pltpu.make_async_remote_copy(
            src_ref=src,
            dst_ref=dst,
            send_sem=send_sem,
            recv_sem=recv_sem,
            device_id={"seq": p},
            device_id_type=MESH,
        )

    def all_of(ref, send_sem, recv_sem):
        return to_seq(ref, ref, send_sem, recv_sem, peers[0])

    def keys_to(p):
        for kind, ref in enumerate((vk, vv)):
            to_seq(ref.at[:, cols_of(p)], kv.at[kind, rows_of(me)], kv_send, kv_recv, p).start()

    def send_queries(r):
        here = pl.ds(*cuts[r])
        for p in peers:
            to_seq(vq.at[here, cols_of(p)], q_all.at[slot(me, r)], q_send, q_recv.at[r], p).start()

    def audio_hop(step, way):
        shard = lax.rem(me - way * step + seq, seq)
        here = audio_rows_of(shard)
        return to_seq(
            audio.at[:, here],
            audio.at[:, here],
            audio_send.at[(way + 1) // 2],
            audio_recv.at[shard],
            lax.rem(me + way + seq, seq),
        )

    def on_line(step, way):
        source, target = me - way * step, me + way
        return (source >= 0) & (source < seq) & (target >= 0) & (target < seq)

    def pass_audio(step):
        for way in (1, -1):

            @pl.when(on_line(step, way))
            def _():
                copy = audio_hop(step, way)
                if step:
                    copy.wait_recv()
                    audio_hop(step - 1, way).wait_send()
                copy.start()

    def end_audio():
        for step in range(1, seq):
            for way in (1, -1):
                source, target = me - way * step, me + way
                last = (target < 0) | (target >= seq)

                @pl.when((source >= 0) & (source < seq) & last)
                def _():
                    audio_hop(step, way).wait_recv()

    def pass_token(way):
        index = (way + 1) // 2

        @pl.when((me - 2 * way >= 0) & (me - 2 * way < seq))
        def _():
            pl.semaphore_wait(token.at[index], 1)

        @pl.when(
            (me - way >= 0) & (me - way < seq) & (me + way >= 0) & (me + way < seq)
        )
        def _():
            pl.semaphore_signal(
                token.at[index], inc=1, device_id={"seq": me + way}, device_id_type=MESH
            )

    local_done(audio.at[:, audio_rows_of(0)], audio_own)
    pass_audio(0)
    keys_to(peers[0])
    with jax.named_scope("tokens"):
        pass_token(1)
        pass_token(-1)
    for p in peers[1:]:
        keys_to(p)
    with jax.named_scope("pass1"):
        pass_audio(1)
    for r in range(groups):
        send_queries(r)
    weight_copy = pltpu.make_async_copy(weight, weight_v, weight_sem)
    weight_copy.start()

    def wait_keys():
        local_done(kv.at[:, rows_of(0)], own_kv)
        local_done(q_all.at[rows_of(0)], own_q)
        all_of(kv.at[:, pl.ds(0, (seq - 1) * rows)], kv_send, kv_recv).wait_recv()

    def attend_rows(r):
        start, size = cuts[r]
        all_of(q_all.at[pl.ds(0, (seq - 1) * size)], q_send, q_recv.at[r]).wait_recv()
        block = pl.ds(seq * start, seq * size)
        for h in range(share):
            cols = slice(h * HD, (h + 1) * HD)
            _, row_sum, numerator = softmax_parts(q_all[block, cols], kv[0, :, cols], kv[1, :, cols])
            heads_out[block, cols] = (numerator / row_sum).astype(jnp.bfloat16)
        here = pl.ds(start, size)
        for p in peers:
            to_seq(heads_out.at[slot(p, r)], gathered.at[me, here], out_send, out_recv.at[r], p).start()
        gathered[me, here] = heads_out[slot(me, r)]

    def cross_audio():
        local_done(cross_v, cross_sem)
        end_audio()
        lane = lax.broadcasted_iota(jnp.int32, (seq * audio_rows, HD), 1)
        held = jnp.zeros((seq * audio_rows, HD), jnp.float32)
        for c in range(cross_heads):
            cols = slice(c * HD, (c + 1) * HD)
            highest, row_sum, numerator = softmax_parts(
                audio[2, :, cols], cross_v[1, :, cols], cross_v[2, :, cols]
            )
            held = jnp.where(lane == c, highest, held)
            held = jnp.where(lane == cross_heads + c, row_sum, held)
            partial[:, cols] = numerator.astype(jnp.bfloat16)
        stats[...] = held

    def cross_video():
        for c in range(cross_heads):
            cols = slice(c * HD, (c + 1) * HD)
            _, row_sum, numerator = softmax_parts(
                cross_v[0, :, cols], audio[0, :, cols], audio[1, :, cols]
            )
            vcross_ref[:, cols] = (numerator / row_sum).astype(jnp.bfloat16)

    def cross_send():
        for p in peers:
            theirs = audio_rows_of(p)
            to_seq(partial.at[theirs], partial_in.at[me], part_send, part_recv, p).start()
            to_seq(stats.at[theirs], stats_in.at[me], stat_send, stat_recv, p).start()

    def cross_finish():
        all_of(partial_in.at[pl.ds(0, seq - 1)], part_send, part_recv).wait_recv()
        all_of(stats_in.at[pl.ds(0, seq - 1)], stat_send, stat_recv).wait_recv()
        my_audio = audio_rows_of(me)
        held = [stats[my_audio, :]] + [stats_in[p] for p in peers]
        for c in range(cross_heads):
            cols = slice(c * HD, (c + 1) * HD)
            parts = [partial[my_audio, cols]] + [partial_in[p, :, cols] for p in peers]
            tops = [s[:, c : c + 1] for s in held]
            sums = [s[:, cross_heads + c : cross_heads + c + 1] for s in held]
            highest = functools.reduce(jnp.maximum, tops)
            factors = [jnp.exp(t - highest) for t in tops]
            row_sum = sum(f * s for f, s in zip(factors, sums))
            numerator = sum(f * n.astype(jnp.float32) for f, n in zip(factors, parts))
            across_ref[:, cols] = (numerator / row_sum).astype(jnp.bfloat16)

    def product(attended, d, side, j):
        target = far_chips[d] * 2 + (core if side else 1 - core)
        cols = pl.ds(pl.multiple_of(target * width + j * WIDE, WIDE), WIDE)
        return jnp.dot(attended, weight_v[:, cols], preferred_element_type=jnp.float32)

    def pair_copy(r, d):
        here = pl.ds(*cuts[r])
        return pltpu.make_async_remote_copy(
            src_ref=pair_out.at[d, here],
            dst_ref=pair_in.at[d, here],
            send_sem=pair_send,
            recv_sem=pair_recv.at[r, d - 1],
            device_id={"tensor": sibling},
            device_id_type=MESH,
        )

    def far_copy(r, d):
        here = pl.ds(*cuts[r])
        return pltpu.make_async_remote_copy(
            src_ref=far_out.at[d - 1, here],
            dst_ref=far_in.at[d - 1, here],
            send_sem=far_send,
            recv_sem=far_recv.at[r, d - 1],
            device_id={"tensor": far_chips[d] * 2 + core},
            device_id_type=MESH,
        )

    home_copy = pltpu.make_async_remote_copy(
        src_ref=pair_out.at[0],
        dst_ref=pair_in.at[0],
        send_sem=pair_send,
        recv_sem=home_recv,
        device_id={"tensor": sibling},
        device_id_type=MESH,
    )
    blocks = [slice(j * WIDE, (j + 1) * WIDE) for j in range(pieces)]

    def share_rows(r):
        here = pl.ds(*cuts[r])
        all_of(gathered.at[pl.ds(0, seq - 1), here], out_send, out_recv.at[r]).wait_recv()
        attended = jnp.concatenate([gathered[p, here] for p in range(seq)], axis=1)
        if r == 0:
            weight_copy.wait()
        for d in range(1, chips):
            for j, block in enumerate(blocks):
                pair_out[d, here, block] = product(attended, d, 0, j).astype(jnp.bfloat16)
            pair_copy(r, d).start()
        for d in range(1, chips):
            for j, block in enumerate(blocks):
                mine[d - 1, here, block] = product(attended, d, 1, j)
        for d in range(1, chips):
            pair_copy(r, d).wait_recv()
            far_out[d - 1, here] = (mine[d - 1, here] + pair_in[d, here].astype(jnp.float32)).astype(
                jnp.bfloat16
            )
            far_copy(r, d).start()

    def keep_rows():
        attended = jnp.concatenate([gathered[p] for p in range(seq)], axis=1)
        for j, block in enumerate(blocks):
            pair_out[0, :, block] = product(attended, 0, 0, j).astype(jnp.bfloat16)
        home_copy.start()
        stream_copy.wait()
        for j, block in enumerate(blocks):
            kept[:, block] = product(attended, 0, 1, j) + stream_v[:, block].astype(jnp.float32)

    def close_rows(r):
        here = pl.ds(*cuts[r])
        value = kept[here] + pair_in[0, here].astype(jnp.float32)
        for d in range(1, chips):
            far_copy(r, d).wait_recv()
            value = value + far_in[d - 1, here].astype(jnp.float32)
        next_ref[here] = value.astype(jnp.bfloat16)

    def settle():
        all_of(kv.at[:, pl.ds(0, (seq - 1) * rows)], kv_send, kv_recv).wait_send()
        all_of(q_all.at[pl.ds(0, (seq - 1) * rows)], q_send, q_recv.at[0]).wait_send()
        all_of(heads_out.at[pl.ds(0, (seq - 1) * rows)], out_send, out_recv.at[0]).wait_send()
        all_of(partial.at[pl.ds(0, (seq - 1) * audio_rows)], part_send, part_recv).wait_send()
        all_of(stats.at[pl.ds(0, (seq - 1) * audio_rows)], stat_send, stat_recv).wait_send()
        for way in (1, -1):
            for step in range(seq - 1):

                @pl.when(on_line(step, way) & jnp.logical_not(on_line(step + 1, way)))
                def _():
                    audio_hop(step, way).wait_send()

        all_of(pair_out, pair_send, pair_recv.at[0, 0]).wait_send()
        if chips > 1:
            all_of(far_out, far_send, far_recv.at[0, 0]).wait_send()

    with jax.named_scope("wait_keys"):
        wait_keys()
    for r in range(groups):
        with jax.named_scope(f"attend{r}"):
            attend_rows(r)
        if r == 0:
            with jax.named_scope("pass2"):
                for step in range(2, seq - 1):
                    pass_audio(step)
    with jax.named_scope("cross_audio"):
        cross_audio()
    with jax.named_scope("cross_video"):
        cross_video()
    for r in range(groups):
        if r == groups - 1:
            with jax.named_scope("cross_send"):
                cross_send()
        with jax.named_scope(f"share{r}"):
            share_rows(r)
    with jax.named_scope("keep"):
        keep_rows()
    with jax.named_scope("cross_finish"):
        cross_finish()
    with jax.named_scope("wait_home"):
        home_copy.wait_recv()
    for r in range(groups):
        with jax.named_scope(f"close{r}"):
            close_rows(r)
    with jax.named_scope("settle"):
        settle()


def write_out(*refs):
    half = len(refs) // 2
    for src, dst in zip(refs[:half], refs[half:]):
        dst[...] = src[...]


def fused(seq, tensor, *operands):
    vq, vk, vv, vs, weight, cq, ak, av, aq, ck, cv = operands
    rows, features = vq.shape
    span = features // seq
    audio_rows, cross_width = aq.shape
    chips = tensor // 2
    width = weight.shape[1] // tensor
    groups = len(row_cuts(rows))
    others = max(chips - 1, 1)
    bf16, f32, dma = jnp.bfloat16, jnp.float32, pltpu.SemaphoreType.DMA
    shapes = tuple(jax.ShapeDtypeStruct(x.shape, bf16) for x in (vs, cq, aq))
    whole = pl.BlockSpec(memory_space=pltpu.VMEM)
    results = pl.pallas_call(
        functools.partial(block_kernel, seq, tensor),
        out_shape=tuple(pltpu.VMEM(x.shape, bf16) for x in (vs, cq, aq)),
        in_specs=[pl.BlockSpec(memory_space=pltpu.HBM)] * 11,
        out_specs=(whole,) * 3,
        scratch_shapes=[
            pltpu.VMEM((2, seq * rows, span), bf16),
            pltpu.VMEM((seq * rows, span), bf16),
            pltpu.VMEM((seq * rows, span), bf16),
            pltpu.VMEM((seq, rows, span), bf16),
            pltpu.VMEM((3, seq * audio_rows, cross_width), bf16),
            pltpu.VMEM((seq * audio_rows, cross_width), bf16),
            pltpu.VMEM((seq * audio_rows, HD), f32),
            pltpu.VMEM((seq, audio_rows, cross_width), bf16),
            pltpu.VMEM((seq, audio_rows, HD), f32),
            pltpu.VMEM((3, *cq.shape), bf16),
            pltpu.VMEM(vs.shape, bf16),
            pltpu.VMEM(weight.shape, bf16),
            pltpu.VMEM(vs.shape, f32),
            pltpu.VMEM((others, rows, width), f32),
            pltpu.VMEM((chips, rows, width), bf16),
            pltpu.VMEM((chips, rows, width), bf16),
            pltpu.VMEM((others, rows, width), bf16),
            pltpu.VMEM((others, rows, width), bf16),
            pltpu.SemaphoreType.REGULAR((2,)),
            dma(()),
            dma(()),
            dma(()),
            dma((groups,)),
            dma(()),
            dma(()),
            dma(()),
            dma((groups,)),
            dma((2,)),
            dma((seq,)),
            dma(()),
            dma(()),
            dma(()),
            dma(()),
            dma(()),
            dma(()),
            dma(()),
            dma(()),
            dma(()),
            dma((groups, others)),
            dma(()),
            dma(()),
            dma((groups, others)),
        ],
        compiler_params=pltpu.CompilerParams(
            collective_id=0, has_side_effects=True, vmem_limit_bytes=60000000
        ),
    )(*operands)
    return pl.pallas_call(
        write_out,
        out_shape=shapes,
        in_specs=[whole] * 3,
        out_specs=(whole,) * 3,
        compiler_params=pltpu.CompilerParams(vmem_limit_bytes=8 * 2**20),
    )(*results)


def fits(mesh, operands):
    seq, tensor = mesh.shape["seq"], mesh.shape["tensor"]
    vq, weight, cq, aq = operands[0], operands[4], operands[5], operands[8]
    return (
        seq > 1
        and (vq.shape[1] // HD) % seq == 0
        and tensor % 2 == 0
        and (weight.shape[1] // tensor) % WIDE == 0
        and aq.shape[0] % 16 == 0
        and vq.shape[0] % 16 == 0
        and 2 * (cq.shape[1] // HD) <= HD
        and weight.size * 2 <= 10 * 2**20
        and vq.shape[0] <= 128
        and seq <= 8
    )


def solution(mesh):
    def step(*operands):
        if fits(mesh, operands):
            return fused(mesh.shape["seq"], mesh.shape["tensor"], *operands)
        return local(*operands)

    in_specs = (
        P(("groups", "seq"), "tensor"),
        P(("groups", "seq"), "tensor"),
        P(("groups", "seq"), "tensor"),
        P(("groups", "seq"), "tensor"),
        P("tensor", None),
        P(("groups", "seq"), "tensor"),
        P(("groups", "seq"), "tensor"),
        P(("groups", "seq"), "tensor"),
        P(("groups", "seq"), "tensor"),
        P(("groups", "seq"), "tensor"),
        P(("groups", "seq"), "tensor"),
    )
    out_specs = (
        P(("groups", "seq"), "tensor"),
        P(("groups", "seq"), "tensor"),
        P(("groups", "seq"), "tensor"),
    )
    return jax.shard_map(step, mesh=mesh, in_specs=in_specs, out_specs=out_specs, check_vma=False)
```

time: 43.6 us -> 41.1 us (0.943)
  Pallas kernels: 42.8 us -> 40.3 us
    pallas_call x1, Pallas kernels: 42 us -> 39.5 us  [fused(): pl.pallas_call(functools.partial(block_kernel, seq, tensor), out_shape=tu...]
where the time goes in v1:
time: 41.1 us; the launch traced here: 40.9 us
  Pallas kernels  40.3 us (98%)
  between operations  0.64 us (2%)
    pallas_call x1, Pallas kernels, fused(): pl.pallas_call(functools.partial(block_kernel, seq, tensor), out_shape=tu...  39.5 us

profile of v1, /device:TPU:0, one launch (start us, length us, event | category | flops | bytes accessed | tf_op | source)
XLA Modules:
  0.0 40.9 jit_solution(5407288786763304486)
XLA Ops:
  0.6 39.5 %shard_map.130 = (bf16[128,1024]{1,0:T(8,128)(2,1)S(1)}, bf16[128,512]{1,0:T(8,128)(2,1)S(1)}, bf16[16,512]{1,0:T(8,128)(2,1)S(1)}) custom-call(bf16[128,1024]{1,0:T(8,128)(2,1)} %vq.1, bf16[128,1024]{1,0:T(8,128)(2,1)} %vk.1, bf16[128,1024]{1,0:T(8,128)(2,1)} %vv.1, bf16[128,1024]{1,0:T(8,128)(2,1)} %vs.1, bf16[1024,4096]{1,0:T(8,128)(2,1)} %weight.1, ...), custom_call_target="tpu_custom_call" | custom-call | tf_op jit(solution)/shard_map/pallas_call | solution.py:560
  40.1 0.8 %shard_map.131 = (bf16[128,1024]{1,0:T(8,128)(2,1)}, bf16[128,512]{1,0:T(8,128)(2,1)}, bf16[16,512]{1,0:T(8,128)(2,1)}) custom-call(bf16[128,1024]{1,0:T(8,128)(2,1)S(1)} %get-tuple-element.6.refs_0_, bf16[128,512]{1,0:T(8,128)(2,1)S(1)} %get-tuple-element.7.refs_1_, bf16[16,512]{1,0:T(8,128)(2,1)S(1)} %get-tuple-element.8.refs_2_), custom_call_target="tpu_custom_call" | custom-call | tf_op jit(solution)/shard_map/pallas_call | solution.py:613

commit v2 on v1

--- a/solution.py
+++ b/solution.py
@@ -180,6 +180,7 @@
     far_out,
     far_in,
     token,
+    beside,
     kv_send,
     kv_recv,
     q_send,
@@ -278,13 +279,13 @@
     def all_of(ref, send_sem, recv_sem):
         return to_seq(ref, ref, send_sem, recv_sem, peers[0])
 
-    def keys_to(p):
-        for kind, ref in enumerate((vk, vv)):
+    def keys_to(p, kinds=(0, 1)):
+        for kind, ref in zip(kinds, (vk, vv)[kinds[0] :]):
             to_seq(ref.at[:, cols_of(p)], kv.at[kind, rows_of(me)], kv_send, kv_recv, p).start()
 
     def send_queries(r):
         here = pl.ds(*cuts[r])
-        for p in peers:
+        for p in peers[::-1]:
             to_seq(vq.at[here, cols_of(p)], q_all.at[slot(me, r)], q_send, q_recv.at[r], p).start()
 
     def audio_hop(step, way):
@@ -339,17 +340,32 @@
             )
 
     local_done(audio.at[:, audio_rows_of(0)], audio_own)
-    pass_audio(0)
-    keys_to(peers[0])
-    with jax.named_scope("tokens"):
+    def run(name, f, *args):
+        with jax.named_scope(name):
+            f(*args)
+
+    def tokens():
         pass_token(1)
         pass_token(-1)
-    for p in peers[1:]:
-        keys_to(p)
-    with jax.named_scope("pass1"):
-        pass_audio(1)
-    for r in range(groups):
-        send_queries(r)
+
+    def late_audio():
+        for step in range(2, seq - 1):
+            pass_audio(step)
+
+    def meet():
+        pl.semaphore_signal(
+            beside.at[0], inc=1, device_id={"tensor": sibling}, device_id_type=MESH
+        )
+        pl.semaphore_wait(beside.at[0], 1)
+
+    run("p0", pass_audio, 0)
+    run("K0", keys_to, peers[0])
+    run("tok", tokens)
+    run("sib", meet)
+    run("K1", keys_to, peers[1])
+    run("K2", keys_to, peers[2])
+    run("p1", pass_audio, 1)
+    run("q0", send_queries, 0)
     weight_copy = pltpu.make_async_copy(weight, weight_v, weight_sem)
     weight_copy.start()
 
@@ -367,7 +383,7 @@
             _, row_sum, numerator = softmax_parts(q_all[block, cols], kv[0, :, cols], kv[1, :, cols])
             heads_out[block, cols] = (numerator / row_sum).astype(jnp.bfloat16)
         here = pl.ds(start, size)
-        for p in peers:
+        for p in peers[::-1]:
             to_seq(heads_out.at[slot(p, r)], gathered.at[me, here], out_send, out_recv.at[r], p).start()
         gathered[me, here] = heads_out[slot(me, r)]
 
@@ -466,6 +482,9 @@
         for d in range(1, chips):
             for j, block in enumerate(blocks):
                 mine[d - 1, here, block] = product(attended, d, 1, j)
+
+    def send_far(r):
+        here = pl.ds(*cuts[r])
         for d in range(1, chips):
             pair_copy(r, d).wait_recv()
             far_out[d - 1, here] = (mine[d - 1, here] + pair_in[d, here].astype(jnp.float32)).astype(
@@ -473,11 +492,17 @@
             )
             far_copy(r, d).start()
 
-    def keep_rows():
-        attended = jnp.concatenate([gathered[p] for p in range(seq)], axis=1)
+    def all_heads():
+        return jnp.concatenate([gathered[p] for p in range(seq)], axis=1)
+
+    def give_home():
+        attended = all_heads()
         for j, block in enumerate(blocks):
             pair_out[0, :, block] = product(attended, 0, 0, j).astype(jnp.bfloat16)
         home_copy.start()
+
+    def keep_home():
+        attended = all_heads()
         stream_copy.wait()
         for j, block in enumerate(blocks):
             kept[:, block] = product(attended, 0, 1, j) + stream_v[:, block].astype(jnp.float32)
@@ -507,34 +532,29 @@
         if chips > 1:
             all_of(far_out, far_send, far_recv.at[0, 0]).wait_send()
 
-    with jax.named_scope("wait_keys"):
-        wait_keys()
-    for r in range(groups):
-        with jax.named_scope(f"attend{r}"):
-            attend_rows(r)
-        if r == 0:
-            with jax.named_scope("pass2"):
-                for step in range(2, seq - 1):
-                    pass_audio(step)
-    with jax.named_scope("cross_audio"):
-        cross_audio()
-    with jax.named_scope("cross_video"):
-        cross_video()
-    for r in range(groups):
-        if r == groups - 1:
-            with jax.named_scope("cross_send"):
-                cross_send()
-        with jax.named_scope(f"share{r}"):
-            share_rows(r)
-    with jax.named_scope("keep"):
-        keep_rows()
-    with jax.named_scope("cross_finish"):
-        cross_finish()
-    with jax.named_scope("wait_home"):
-        home_copy.wait_recv()
-    for r in range(groups):
-        with jax.named_scope(f"close{r}"):
-            close_rows(r)
+    run("wk", wait_keys)
+    run("q1", send_queries, 1)
+    run("p2", late_audio)
+    run("a0", attend_rows, 0)
+    run("q2", send_queries, 2)
+    run("a1", attend_rows, 1)
+    run("ca", cross_audio)
+    run("A0", share_rows, 0)
+    run("a2", attend_rows, 2)
+    run("B0", send_far, 0)
+    run("A1", share_rows, 1)
+    run("B1", send_far, 1)
+    run("cs", cross_send)
+    run("A2", share_rows, 2)
+    run("k0", give_home)
+    run("B2", send_far, 2)
+    run("cv", cross_video)
+    run("k1", keep_home)
+    run("cf", cross_finish)
+    run("h", home_copy.wait_recv)
+    run("c0", close_rows, 0)
+    run("c1", close_rows, 1)
+    run("c2", close_rows, 2)
     with jax.named_scope("settle"):
         settle()
 
@@ -582,6 +602,7 @@
             pltpu.VMEM((others, rows, width), bf16),
             pltpu.VMEM((others, rows, width), bf16),
             pltpu.SemaphoreType.REGULAR((2,)),
+            pltpu.SemaphoreType.REGULAR((1,)),
             dma(()),
             dma(()),
             dma(()),

time: 41.1 us -> 39.6 us (0.964)
  Pallas kernels: 40.3 us -> 38.8 us
    pallas_call x1, Pallas kernels: 39.5 us -> 38 us  [fused(): pl.pallas_call(functools.partial(block_kernel, seq, tensor), out_shape=tu...]
where the time goes in v2:
time: 39.6 us; the launch traced here: 39.5 us
  Pallas kernels  38.8 us (98%)
  between operations  0.64 us (2%)
    pallas_call x1, Pallas kernels, fused(): pl.pallas_call(functools.partial(block_kernel, seq, tensor), out_shape=tu...  38 us

profile of v2, /device:TPU:0, one launch (start us, length us, event | category | flops | bytes accessed | tf_op | source)
XLA Modules:
  0.0 39.5 jit_solution(15626942394659172529)
XLA Ops:
  0.6 38.0 %shard_map.130 = (bf16[128,1024]{1,0:T(8,128)(2,1)S(1)}, bf16[128,512]{1,0:T(8,128)(2,1)S(1)}, bf16[16,512]{1,0:T(8,128)(2,1)S(1)}) custom-call(bf16[128,1024]{1,0:T(8,128)(2,1)} %vq.1, bf16[128,1024]{1,0:T(8,128)(2,1)} %vk.1, bf16[128,1024]{1,0:T(8,128)(2,1)} %vv.1, bf16[128,1024]{1,0:T(8,128)(2,1)} %vs.1, bf16[1024,4096]{1,0:T(8,128)(2,1)} %weight.1, ...), custom_call_target="tpu_custom_call" | custom-call | tf_op jit(solution)/shard_map/pallas_call | solution.py:580
  38.7 0.8 %shard_map.131 = (bf16[128,1024]{1,0:T(8,128)(2,1)}, bf16[128,512]{1,0:T(8,128)(2,1)}, bf16[16,512]{1,0:T(8,128)(2,1)}) custom-call(bf16[128,1024]{1,0:T(8,128)(2,1)S(1)} %get-tuple-element.6.refs_0_, bf16[128,512]{1,0:T(8,128)(2,1)S(1)} %get-tuple-element.7.refs_1_, bf16[16,512]{1,0:T(8,128)(2,1)S(1)} %get-tuple-element.8.refs_2_), custom_call_target="tpu_custom_call" | custom-call | tf_op jit(solution)/shard_map/pallas_call | solution.py:634

commit v3 on v2

--- a/solution.py
+++ b/solution.py
@@ -113,6 +113,7 @@
 NT = (((1,), (1,)), ((), ()))
 WIDE = 512
 SHARES = (3, 3, 2)
+SPLIT = True
 
 
 def softmax_parts(queries, keyset, values):
@@ -167,14 +168,13 @@
     gathered,
     audio,
     partial,
-    stats,
     partial_in,
-    stats_in,
     cross_v,
     stream_v,
     weight_v,
     kept,
     mine,
+    other,
     pair_out,
     pair_in,
     far_out,
@@ -189,13 +189,12 @@
     own_q,
     out_send,
     out_recv,
+    out_last,
     audio_send,
     audio_recv,
     audio_own,
     part_send,
     part_recv,
-    stat_send,
-    stat_recv,
     cross_sem,
     stream_sem,
     weight_sem,
@@ -281,21 +280,22 @@
 
     def keys_to(p, kinds=(0, 1)):
         for kind, ref in zip(kinds, (vk, vv)[kinds[0] :]):
-            to_seq(ref.at[:, cols_of(p)], kv.at[kind, rows_of(me)], kv_send, kv_recv, p).start()
+            to_seq(ref.at[:, cols_of(p)], kv.at[kind, rows_of(me)], kv_send, kv_recv.at[me], p).start()
 
     def send_queries(r):
         here = pl.ds(*cuts[r])
         for p in peers[::-1]:
             to_seq(vq.at[here, cols_of(p)], q_all.at[slot(me, r)], q_send, q_recv.at[r], p).start()
 
-    def audio_hop(step, way):
+    def audio_hop(step, way, part):
         shard = lax.rem(me - way * step + seq, seq)
         here = audio_rows_of(shard)
+        block = audio.at[2, here] if part else audio.at[pl.ds(0, 2), here]
         return to_seq(
-            audio.at[:, here],
-            audio.at[:, here],
-            audio_send.at[(way + 1) // 2],
-            audio_recv.at[shard],
+            block,
+            block,
+            audio_send.at[part, (way + 1) // 2, step],
+            audio_recv.at[part, shard],
             lax.rem(me + way + seq, seq),
         )
 
@@ -303,18 +303,40 @@
         source, target = me - way * step, me + way
         return (source >= 0) & (source < seq) & (target >= 0) & (target < seq)
 
-    def pass_audio(step):
+    def pass_audio(step, part):
         for way in (1, -1):
 
             @pl.when(on_line(step, way))
             def _():
-                copy = audio_hop(step, way)
+                copy = audio_hop(step, way, part)
                 if step:
                     copy.wait_recv()
-                    audio_hop(step - 1, way).wait_send()
                 copy.start()
 
-    def end_audio():
+    def crosses(way):
+        return me == (seq // 2 - 1 if way > 0 else seq // 2)
+
+    def some_audio(steps, chosen):
+        for step in steps:
+            for way in (1, -1):
+
+                @pl.when(on_line(step, way) & chosen(step, way))
+                def _():
+                    copy = audio_hop(step, way, 0)
+                    if step:
+                        copy.wait_recv()
+                    copy.start()
+
+    def early_part():
+        some_audio((0,), lambda step, way: jnp.logical_not(crosses(way)))
+
+    def cross_part():
+        some_audio((0, 1), lambda step, way: crosses(way))
+
+    def relay_part():
+        some_audio(range(1, seq - 1), lambda step, way: (step > 1) | jnp.logical_not(crosses(way)))
+
+    def end_audio(part):
         for step in range(1, seq):
             for way in (1, -1):
                 source, target = me - way * step, me + way
@@ -322,35 +344,48 @@
 
                 @pl.when((source >= 0) & (source < seq) & last)
                 def _():
-                    audio_hop(step, way).wait_recv()
-
-    def pass_token(way):
-        index = (way + 1) // 2
-
-        @pl.when((me - 2 * way >= 0) & (me - 2 * way < seq))
-        def _():
-            pl.semaphore_wait(token.at[index], 1)
-
-        @pl.when(
-            (me - way >= 0) & (me - way < seq) & (me + way >= 0) & (me + way < seq)
-        )
-        def _():
-            pl.semaphore_signal(
-                token.at[index], inc=1, device_id={"seq": me + way}, device_id_type=MESH
-            )
+                    audio_hop(step, way, part).wait_recv()
+
+    def token_to(way):
+        pl.semaphore_signal(
+            token.at[(way + 1) // 2], inc=1, device_id={"seq": me + way}, device_id_type=MESH
+        )
+
+    def within(p):
+        return (p >= 0) & (p < seq)
+
+    def first_tokens():
+        for way in (1, -1):
+
+            @pl.when(within(me - way) & jnp.logical_not(within(me - 2 * way)) & within(me + way))
+            def _():
+                token_to(way)
+
+    def tokens():
+        for way in (1, -1):
+
+            @pl.when(within(me - 2 * way))
+            def _():
+                pl.semaphore_wait(token.at[(way + 1) // 2], 1)
+
+            @pl.when(within(me - 2 * way) & within(me + way))
+            def _():
+                token_to(way)
 
     local_done(audio.at[:, audio_rows_of(0)], audio_own)
+    def keys_from(p):
+        all_of(kv.at[:, rows_of(0)], kv_send, kv_recv.at[p]).wait_recv()
+
+    def first_keys():
+        keys_from(peers[0])
+
     def run(name, f, *args):
         with jax.named_scope(name):
             f(*args)
 
-    def tokens():
-        pass_token(1)
-        pass_token(-1)
-
-    def late_audio():
+    def late_audio(part):
         for step in range(2, seq - 1):
-            pass_audio(step)
+            pass_audio(step, part)
 
     def meet():
         pl.semaphore_signal(
@@ -358,13 +393,15 @@
         )
         pl.semaphore_wait(beside.at[0], 1)
 
-    run("p0", pass_audio, 0)
+    run("p0", pass_audio, 0, 1)
     run("K0", keys_to, peers[0])
+    run("tk1", first_tokens)
     run("tok", tokens)
     run("sib", meet)
     run("K1", keys_to, peers[1])
     run("K2", keys_to, peers[2])
-    run("p1", pass_audio, 1)
+    run("PE", early_part)
+    run("p1", pass_audio, 1, 1)
     run("q0", send_queries, 0)
     weight_copy = pltpu.make_async_copy(weight, weight_v, weight_sem)
     weight_copy.start()
@@ -372,7 +409,8 @@
     def wait_keys():
         local_done(kv.at[:, rows_of(0)], own_kv)
         local_done(q_all.at[rows_of(0)], own_q)
-        all_of(kv.at[:, pl.ds(0, (seq - 1) * rows)], kv_send, kv_recv).wait_recv()
+        for p in peers[1:]:
+            keys_from(p)
 
     def attend_rows(r):
         start, size = cuts[r]
@@ -384,12 +422,16 @@
             heads_out[block, cols] = (numerator / row_sum).astype(jnp.bfloat16)
         here = pl.ds(start, size)
         for p in peers[::-1]:
-            to_seq(heads_out.at[slot(p, r)], gathered.at[me, here], out_send, out_recv.at[r], p).start()
+            sem = out_last.at[me] if SPLIT and r == groups - 1 else out_recv.at[r]
+            to_seq(heads_out.at[slot(p, r)], gathered.at[me, here], out_send, sem, p).start()
         gathered[me, here] = heads_out[slot(me, r)]
+
+    def upper(value):
+        return value.astype(jnp.bfloat16).astype(jnp.float32)
 
     def cross_audio():
         local_done(cross_v, cross_sem)
-        end_audio()
+        end_audio(1)
         lane = lax.broadcasted_iota(jnp.int32, (seq * audio_rows, HD), 1)
         held = jnp.zeros((seq * audio_rows, HD), jnp.float32)
         for c in range(cross_heads):
@@ -397,12 +439,14 @@
             highest, row_sum, numerator = softmax_parts(
                 audio[2, :, cols], cross_v[1, :, cols], cross_v[2, :, cols]
             )
-            held = jnp.where(lane == c, highest, held)
-            held = jnp.where(lane == cross_heads + c, row_sum, held)
+            for i, value in enumerate((highest, row_sum)):
+                held = jnp.where(lane == 2 * (2 * c + i), upper(value), held)
+                held = jnp.where(lane == 2 * (2 * c + i) + 1, value - upper(value), held)
             partial[:, cols] = numerator.astype(jnp.bfloat16)
-        stats[...] = held
+        partial[:, cross_heads * HD :] = held.astype(jnp.bfloat16)
 
     def cross_video():
+        end_audio(0)
         for c in range(cross_heads):
             cols = slice(c * HD, (c + 1) * HD)
             _, row_sum, numerator = softmax_parts(
@@ -414,18 +458,22 @@
         for p in peers:
             theirs = audio_rows_of(p)
             to_seq(partial.at[theirs], partial_in.at[me], part_send, part_recv, p).start()
-            to_seq(stats.at[theirs], stats_in.at[me], stat_send, stat_recv, p).start()
 
     def cross_finish():
         all_of(partial_in.at[pl.ds(0, seq - 1)], part_send, part_recv).wait_recv()
-        all_of(stats_in.at[pl.ds(0, seq - 1)], stat_send, stat_recv).wait_recv()
         my_audio = audio_rows_of(me)
-        held = [stats[my_audio, :]] + [stats_in[p] for p in peers]
+        stat_cols = slice(cross_heads * HD, (cross_heads + 1) * HD)
+        held = [partial[my_audio, stat_cols]] + [partial_in[p, :, stat_cols] for p in peers]
+        held = [value.astype(jnp.float32) for value in held]
+
+        def stat(s, i):
+            return s[:, 2 * i : 2 * i + 1] + s[:, 2 * i + 1 : 2 * i + 2]
+
         for c in range(cross_heads):
             cols = slice(c * HD, (c + 1) * HD)
             parts = [partial[my_audio, cols]] + [partial_in[p, :, cols] for p in peers]
-            tops = [s[:, c : c + 1] for s in held]
-            sums = [s[:, cross_heads + c : cross_heads + c + 1] for s in held]
+            tops = [stat(s, 2 * c) for s in held]
+            sums = [stat(s, 2 * c + 1) for s in held]
             highest = functools.reduce(jnp.maximum, tops)
             factors = [jnp.exp(t - highest) for t in tops]
             row_sum = sum(f * s for f, s in zip(factors, sums))
@@ -483,6 +531,34 @@
             for j, block in enumerate(blocks):
                 mine[d - 1, here, block] = product(attended, d, 1, j)
 
+    def share_parts(r):
+        here = pl.ds(*cuts[r])
+
+        def add_part(some, d, side, first):
+            target = far_chips[d] * 2 + (core if side else 1 - core)
+            for j, block in enumerate(blocks):
+                cols = pl.ds(pl.multiple_of(target * width + j * WIDE, WIDE), WIDE)
+                value = sum(
+                    jnp.dot(gathered[p, here], weight_v[cols_of(p), cols], preferred_element_type=jnp.float32)
+                    for p in some
+                )
+                ref = mine if side else other
+                ref[d - 1, here, block] = value if first else ref[d - 1, here, block] + value
+
+        some = [me]
+        for i, p in enumerate(peers):
+            all_of(gathered.at[0, here], out_send, out_last.at[p]).wait_recv()
+            some.append(p)
+            if i == 0 and len(peers) > 1:
+                continue
+            for side in (0, 1):
+                for d in range(1, chips):
+                    add_part(some, d, side, i <= 1)
+                    if side == 0 and i == len(peers) - 1:
+                        pair_out[d, here] = other[d - 1, here].astype(jnp.bfloat16)
+                        pair_copy(r, d).start()
+            some = []
+
     def send_far(r):
         here = pl.ds(*cuts[r])
         for d in range(1, chips):
@@ -516,41 +592,44 @@
         next_ref[here] = value.astype(jnp.bfloat16)
 
     def settle():
-        all_of(kv.at[:, pl.ds(0, (seq - 1) * rows)], kv_send, kv_recv).wait_send()
+        all_of(kv.at[:, pl.ds(0, (seq - 1) * rows)], kv_send, kv_recv.at[0]).wait_send()
         all_of(q_all.at[pl.ds(0, (seq - 1) * rows)], q_send, q_recv.at[0]).wait_send()
         all_of(heads_out.at[pl.ds(0, (seq - 1) * rows)], out_send, out_recv.at[0]).wait_send()
         all_of(partial.at[pl.ds(0, (seq - 1) * audio_rows)], part_send, part_recv).wait_send()
-        all_of(stats.at[pl.ds(0, (seq - 1) * audio_rows)], stat_send, stat_recv).wait_send()
         for way in (1, -1):
             for step in range(seq - 1):
 
-                @pl.when(on_line(step, way) & jnp.logical_not(on_line(step + 1, way)))
+                @pl.when(on_line(step, way))
                 def _():
-                    audio_hop(step, way).wait_send()
+                    for part in (0, 1):
+                        audio_hop(step, way, part).wait_send()
 
         all_of(pair_out, pair_send, pair_recv.at[0, 0]).wait_send()
         if chips > 1:
             all_of(far_out, far_send, far_recv.at[0, 0]).wait_send()
 
+    run("w0", first_keys)
     run("wk", wait_keys)
     run("q1", send_queries, 1)
-    run("p2", late_audio)
+    run("p2", late_audio, 1)
     run("a0", attend_rows, 0)
     run("q2", send_queries, 2)
     run("a1", attend_rows, 1)
     run("ca", cross_audio)
     run("A0", share_rows, 0)
     run("a2", attend_rows, 2)
+    run("PL", cross_part)
     run("B0", send_far, 0)
     run("A1", share_rows, 1)
     run("B1", send_far, 1)
     run("cs", cross_send)
-    run("A2", share_rows, 2)
+    run("PR", relay_part)
+    run("A2", share_parts, 2)
+    run("B2", send_far, 2)
     run("k0", give_home)
-    run("B2", send_far, 2)
-    run("cv", cross_video)
     run("k1", keep_home)
     run("cf", cross_finish)
+    run("cv", cross_video)
     run("h", home_copy.wait_recv)
     run("c0", close_rows, 0)
     run("c1", close_rows, 1)
@@ -588,14 +667,13 @@
             pltpu.VMEM((seq * rows, span), bf16),
             pltpu.VMEM((seq, rows, span), bf16),
             pltpu.VMEM((3, seq * audio_rows, cross_width), bf16),
-            pltpu.VMEM((seq * audio_rows, cross_width), bf16),
-            pltpu.VMEM((seq * audio_rows, HD), f32),
-            pltpu.VMEM((seq, audio_rows, cross_width), bf16),
-            pltpu.VMEM((seq, audio_rows, HD), f32),
+            pltpu.VMEM((seq * audio_rows, cross_width + HD), bf16),
+            pltpu.VMEM((seq, audio_rows, cross_width + HD), bf16),
             pltpu.VMEM((3, *cq.shape), bf16),
             pltpu.VMEM(vs.shape, bf16),
             pltpu.VMEM(weight.shape, bf16),
             pltpu.VMEM(vs.shape, f32),
+            pltpu.VMEM((others, rows, width), f32),
             pltpu.VMEM((others, rows, width), f32),
             pltpu.VMEM((chips, rows, width), bf16),
             pltpu.VMEM((chips, rows, width), bf16),
@@ -604,17 +682,16 @@
             pltpu.SemaphoreType.REGULAR((2,)),
             pltpu.SemaphoreType.REGULAR((1,)),
             dma(()),
-            dma(()),
+            dma((seq,)),
             dma(()),
             dma((groups,)),
             dma(()),
             dma(()),
             dma(()),
             dma((groups,)),
-            dma((2,)),
             dma((seq,)),
-            dma(()),
-            dma(()),
+            dma((2, 2, seq - 1)),
+            dma((2, seq)),
             dma(()),
             dma(()),
             dma(()),
@@ -650,7 +727,7 @@
         and (weight.shape[1] // tensor) % WIDE == 0
         and aq.shape[0] % 16 == 0
         and vq.shape[0] % 16 == 0
-        and 2 * (cq.shape[1] // HD) <= HD
+        and 4 * (cq.shape[1] // HD) <= HD
         and weight.size * 2 <= 10 * 2**20
         and vq.shape[0] <= 128
         and seq <= 8

time: 39.6 us -> 38.1 us (0.962)
  Pallas kernels: 38.8 us -> 37.3 us
    pallas_call x1, Pallas kernels: 38 us -> 36.5 us  [fused(): pl.pallas_call(functools.partial(block_kernel, seq, tensor), out_shape=tu...]
where the time goes in v3:
time: 38.1 us; the launch traced here: 38 us
  Pallas kernels  37.3 us (98%)
  between operations  0.64 us (2%)
    pallas_call x1, Pallas kernels, fused(): pl.pallas_call(functools.partial(block_kernel, seq, tensor), out_shape=tu...  36.5 us
    pallas_call x1, Pallas kernels, fused(): pl.pallas_call(write_out, out_shape=shapes, in_specs=[whole] * 3, out_spe...  0.78 us

profile of v3, /device:TPU:0, one launch (start us, length us, event | category | flops | bytes accessed | tf_op | source)
XLA Modules:
  0.0 38.0 jit_solution(7420243921957513504)
XLA Ops:
  0.6 36.5 %shard_map.130 = (bf16[128,1024]{1,0:T(8,128)(2,1)S(1)}, bf16[128,512]{1,0:T(8,128)(2,1)S(1)}, bf16[16,512]{1,0:T(8,128)(2,1)S(1)}) custom-call(bf16[128,1024]{1,0:T(8,128)(2,1)} %vq.1, bf16[128,1024]{1,0:T(8,128)(2,1)} %vk.1, bf16[128,1024]{1,0:T(8,128)(2,1)} %vv.1, bf16[128,1024]{1,0:T(8,128)(2,1)} %vs.1, bf16[1024,4096]{1,0:T(8,128)(2,1)} %weight.1, ...), custom_call_target="tpu_custom_call" | custom-call | tf_op jit(solution)/shard_map/pallas_call | solution.py:659
  37.2 0.8 %shard_map.131 = (bf16[128,1024]{1,0:T(8,128)(2,1)}, bf16[128,512]{1,0:T(8,128)(2,1)}, bf16[16,512]{1,0:T(8,128)(2,1)}) custom-call(bf16[128,1024]{1,0:T(8,128)(2,1)S(1)} %get-tuple-element.6.refs_0_, bf16[128,512]{1,0:T(8,128)(2,1)S(1)} %get-tuple-element.7.refs_1_, bf16[16,512]{1,0:T(8,128)(2,1)S(1)} %get-tuple-element.8.refs_2_), custom_call_target="tpu_custom_call" | custom-call | tf_op jit(solution)/shard_map/pallas_call | solution.py:711

commit v4 on v3

--- a/solution.py
+++ b/solution.py
@@ -112,7 +112,7 @@
 MESH = pl.DeviceIdType.MESH
 NT = (((1,), (1,)), ((), ()))
 WIDE = 512
-SHARES = (3, 3, 2)
+SHARES = (4, 3, 1)
 SPLIT = True
 
 
@@ -185,8 +185,7 @@
     kv_recv,
     q_send,
     q_recv,
-    own_kv,
-    own_q,
+    own_sem,
     out_send,
     out_recv,
     out_last,
@@ -208,7 +207,7 @@
     span = vq.shape[1] // seq
     share = span // HD
     cross_heads = cq.shape[1] // HD
-    audio_rows = aq.shape[0]
+    audio_rows, cross_width = aq.shape
     chips = tensor // 2
     width = next_ref.shape[1]
     pieces = width // WIDE
@@ -236,9 +235,9 @@
         return pl.ds(pl.multiple_of(seq * start + p * size, 16), size)
 
     for kind, ref in enumerate((vk, vv)):
-        pltpu.make_async_copy(ref.at[:, cols_of(me)], kv.at[kind, rows_of(me)], own_kv).start()
+        pltpu.make_async_copy(ref.at[:, cols_of(me)], kv.at[kind, rows_of(me)], own_sem).start()
     for r in range(groups):
-        pltpu.make_async_copy(vq.at[pl.ds(*cuts[r]), cols_of(me)], q_all.at[slot(me, r)], own_q).start()
+        pltpu.make_async_copy(vq.at[pl.ds(*cuts[r]), cols_of(me)], q_all.at[slot(me, r)], own_sem).start()
     for kind, ref in enumerate((ak, av, aq)):
         pltpu.make_async_copy(ref, audio.at[kind, audio_rows_of(me)], audio_own).start()
     for kind, ref in enumerate((cq, ck, cv)):
@@ -280,7 +279,7 @@
 
     def keys_to(p, kinds=(0, 1)):
         for kind, ref in zip(kinds, (vk, vv)[kinds[0] :]):
-            to_seq(ref.at[:, cols_of(p)], kv.at[kind, rows_of(me)], kv_send, kv_recv.at[me], p).start()
+            to_seq(ref.at[:, cols_of(p)], kv.at[kind, rows_of(me)], kv_send, kv_recv, p).start()
 
     def send_queries(r):
         here = pl.ds(*cuts[r])
@@ -294,7 +293,7 @@
         return to_seq(
             block,
             block,
-            audio_send.at[part, (way + 1) // 2, step],
+            audio_send.at[part],
             audio_recv.at[part, shard],
             lax.rem(me + way + seq, seq),
         )
@@ -373,12 +372,6 @@
                 token_to(way)
 
     local_done(audio.at[:, audio_rows_of(0)], audio_own)
-    def keys_from(p):
-        all_of(kv.at[:, rows_of(0)], kv_send, kv_recv.at[p]).wait_recv()
-
-    def first_keys():
-        keys_from(peers[0])
-
     def run(name, f, *args):
         with jax.named_scope(name):
             f(*args)
@@ -400,17 +393,15 @@
     run("sib", meet)
     run("K1", keys_to, peers[1])
     run("K2", keys_to, peers[2])
+    run("q0", send_queries, 0)
     run("PE", early_part)
     run("p1", pass_audio, 1, 1)
-    run("q0", send_queries, 0)
     weight_copy = pltpu.make_async_copy(weight, weight_v, weight_sem)
     weight_copy.start()
 
     def wait_keys():
-        local_done(kv.at[:, rows_of(0)], own_kv)
-        local_done(q_all.at[rows_of(0)], own_q)
-        for p in peers[1:]:
-            keys_from(p)
+        local_done(kv.at[:, pl.ds(0, rows * 3 // 2)], own_sem)
+        all_of(kv.at[:, pl.ds(0, (seq - 1) * rows)], kv_send, kv_recv).wait_recv()
 
     def attend_rows(r):
         start, size = cuts[r]
@@ -592,23 +583,23 @@
         next_ref[here] = value.astype(jnp.bfloat16)
 
     def settle():
-        all_of(kv.at[:, pl.ds(0, (seq - 1) * rows)], kv_send, kv_recv.at[0]).wait_send()
+        all_of(kv.at[:, pl.ds(0, (seq - 1) * rows)], kv_send, kv_recv).wait_send()
         all_of(q_all.at[pl.ds(0, (seq - 1) * rows)], q_send, q_recv.at[0]).wait_send()
         all_of(heads_out.at[pl.ds(0, (seq - 1) * rows)], out_send, out_recv.at[0]).wait_send()
         all_of(partial.at[pl.ds(0, (seq - 1) * audio_rows)], part_send, part_recv).wait_send()
-        for way in (1, -1):
-            for step in range(seq - 1):
-
-                @pl.when(on_line(step, way))
+        block = audio_rows * cross_width // span
+        for part, count in ((0, 2), (1, 1)):
+            for hops, place_fits in ((1, inner == 0), (seq + 1, inner == 1)):
+
+                @pl.when(place_fits)
                 def _():
-                    for part in (0, 1):
-                        audio_hop(step, way, part).wait_send()
+                    some = heads_out.at[pl.ds(0, hops * count * block)]
+                    all_of(some, audio_send.at[part], audio_recv.at[part, 0]).wait_send()
 
         all_of(pair_out, pair_send, pair_recv.at[0, 0]).wait_send()
         if chips > 1:
             all_of(far_out, far_send, far_recv.at[0, 0]).wait_send()
 
-    run("w0", first_keys)
     run("wk", wait_keys)
     run("q1", send_queries, 1)
     run("p2", late_audio, 1)
@@ -617,8 +608,8 @@
     run("a1", attend_rows, 1)
     run("ca", cross_audio)
     run("A0", share_rows, 0)
+    run("PL", cross_part)
     run("a2", attend_rows, 2)
-    run("PL", cross_part)
     run("B0", send_far, 0)
     run("A1", share_rows, 1)
     run("B1", send_far, 1)
@@ -682,15 +673,14 @@
             pltpu.SemaphoreType.REGULAR((2,)),
             pltpu.SemaphoreType.REGULAR((1,)),
             dma(()),
-            dma((seq,)),
+            dma(()),
             dma(()),
             dma((groups,)),
-            dma(()),
             dma(()),
             dma(()),
             dma((groups,)),
             dma((seq,)),
-            dma((2, 2, seq - 1)),
+            dma((2,)),
             dma((2, seq)),
             dma(()),
             dma(()),
@@ -728,6 +718,8 @@
         and aq.shape[0] % 16 == 0
         and vq.shape[0] % 16 == 0
         and 4 * (cq.shape[1] // HD) <= HD
+        and (aq.size * seq) % (vq.shape[1] * 16) == 0
+        and 2 * (seq + 1) * aq.size <= vq.size
         and weight.size * 2 <= 10 * 2**20
         and vq.shape[0] <= 128
         and seq <= 8

time: 38.1 us -> 37.8 us (level)
  no operation moved by 1% of the time
where the time goes in v4:
time: 37.8 us; the launch traced here: 37.7 us
  Pallas kernels  37 us (98%)
  between operations  0.64 us (2%)
    pallas_call x1, Pallas kernels, fused(): pl.pallas_call(functools.partial(block_kernel, seq, tensor), out_shape=tu...  36.3 us
    pallas_call x1, Pallas kernels, fused(): pl.pallas_call(write_out, out_shape=shapes, in_specs=[whole] * 3, out_spe...  0.78 us

profile of v4, /device:TPU:0, one launch (start us, length us, event | category | flops | bytes accessed | tf_op | source)
XLA Modules:
  0.0 37.7 jit_solution(2886678168184476400)
XLA Ops:
  0.6 36.3 %shard_map.130 = (bf16[128,1024]{1,0:T(8,128)(2,1)S(1)}, bf16[128,512]{1,0:T(8,128)(2,1)S(1)}, bf16[16,512]{1,0:T(8,128)(2,1)S(1)}) custom-call(bf16[128,1024]{1,0:T(8,128)(2,1)} %vq.1, bf16[128,1024]{1,0:T(8,128)(2,1)} %vk.1, bf16[128,1024]{1,0:T(8,128)(2,1)} %vv.1, bf16[128,1024]{1,0:T(8,128)(2,1)} %vs.1, bf16[1024,4096]{1,0:T(8,128)(2,1)} %weight.1, ...), custom_call_target="tpu_custom_call" | custom-call | tf_op jit(solution)/shard_map/pallas_call | solution.py:650
  36.9 0.8 %shard_map.131 = (bf16[128,1024]{1,0:T(8,128)(2,1)}, bf16[128,512]{1,0:T(8,128)(2,1)}, bf16[16,512]{1,0:T(8,128)(2,1)}) custom-call(bf16[128,1024]{1,0:T(8,128)(2,1)S(1)} %get-tuple-element.6.refs_0_, bf16[128,512]{1,0:T(8,128)(2,1)S(1)} %get-tuple-element.7.refs_1_, bf16[16,512]{1,0:T(8,128)(2,1)S(1)} %get-tuple-element.8.refs_2_), custom_call_target="tpu_custom_call" | custom-call | tf_op jit(solution)/shard_map/pallas_call | solution.py:701

commit v5 on v4

--- a/solution.py
+++ b/solution.py
@@ -609,16 +609,44 @@
     run("ca", cross_audio)
     run("A0", share_rows, 0)
     run("PL", cross_part)
+    @pl.when(core == 0)
+    def _():
+        run("B0", send_far, 0)
+
     run("a2", attend_rows, 2)
-    run("B0", send_far, 0)
+    @pl.when(core == 1)
+    def _():
+        run("B0", send_far, 0)
+
+    @pl.when(core == 1)
+    def _():
+        run("PR", relay_part)
+
     run("A1", share_rows, 1)
     run("B1", send_far, 1)
+    @pl.when(core == 0)
+    def _():
+        run("PR", relay_part)
+
     run("cs", cross_send)
-    run("PR", relay_part)
     run("A2", share_parts, 2)
+    @pl.when(core == 1)
+    def _():
+        run("k0", give_home)
+
+    @pl.when(core == 1)
+    def _():
+        run("k1", keep_home)
+
     run("B2", send_far, 2)
-    run("k0", give_home)
-    run("k1", keep_home)
+    @pl.when(core == 0)
+    def _():
+        run("k0", give_home)
+
+    @pl.when(core == 0)
+    def _():
+        run("k1", keep_home)
+
     run("cf", cross_finish)
     run("cv", cross_video)
     run("h", home_copy.wait_recv)

time: 37.8 us -> 37.7 us (level)
  no operation moved by 1% of the time
where the time goes in v5:
time: 37.7 us; the launch traced here: 37.6 us
  Pallas kernels  36.9 us (98%)
  between operations  0.64 us (2%)
    pallas_call x1, Pallas kernels, fused(): pl.pallas_call(functools.partial(block_kernel, seq, tensor), out_shape=tu...  36.2 us
    pallas_call x1, Pallas kernels, fused(): pl.pallas_call(write_out, out_shape=shapes, in_specs=[whole] * 3, out_spe...  0.78 us

profile of v5, /device:TPU:0, one launch (start us, length us, event | category | flops | bytes accessed | tf_op | source)
XLA Modules:
  0.0 37.6 jit_solution(6596349103170789940)
XLA Ops:
  0.6 36.2 %shard_map.130 = (bf16[128,1024]{1,0:T(8,128)(2,1)S(1)}, bf16[128,512]{1,0:T(8,128)(2,1)S(1)}, bf16[16,512]{1,0:T(8,128)(2,1)S(1)}) custom-call(bf16[128,1024]{1,0:T(8,128)(2,1)} %vq.1, bf16[128,1024]{1,0:T(8,128)(2,1)} %vk.1, bf16[128,1024]{1,0:T(8,128)(2,1)} %vv.1, bf16[128,1024]{1,0:T(8,128)(2,1)} %vs.1, bf16[1024,4096]{1,0:T(8,128)(2,1)} %weight.1, ...), custom_call_target="tpu_custom_call" | custom-call | tf_op jit(solution)/shard_map/pallas_call | solution.py:678
  36.8 0.8 %shard_map.131 = (bf16[128,1024]{1,0:T(8,128)(2,1)}, bf16[128,512]{1,0:T(8,128)(2,1)}, bf16[16,512]{1,0:T(8,128)(2,1)}) custom-call(bf16[128,1024]{1,0:T(8,128)(2,1)S(1)} %get-tuple-element.6.refs_0_, bf16[128,512]{1,0:T(8,128)(2,1)S(1)} %get-tuple-element.7.refs_1_, bf16[16,512]{1,0:T(8,128)(2,1)S(1)} %get-tuple-element.8.refs_2_), custom_call_target="tpu_custom_call" | custom-call | tf_op jit(solution)/shard_map/pallas_call | solution.py:729

commit v6 on v5

--- a/solution.py
+++ b/solution.py
@@ -431,8 +431,10 @@
                 audio[2, :, cols], cross_v[1, :, cols], cross_v[2, :, cols]
             )
             for i, value in enumerate((highest, row_sum)):
-                held = jnp.where(lane == 2 * (2 * c + i), upper(value), held)
-                held = jnp.where(lane == 2 * (2 * c + i) + 1, value - upper(value), held)
+                for k in range(3):
+                    piece = upper(value)
+                    held = jnp.where(lane == 3 * (2 * c + i) + k, piece, held)
+                    value = value - piece
             partial[:, cols] = numerator.astype(jnp.bfloat16)
         partial[:, cross_heads * HD :] = held.astype(jnp.bfloat16)
 
@@ -458,7 +460,7 @@
         held = [value.astype(jnp.float32) for value in held]
 
         def stat(s, i):
-            return s[:, 2 * i : 2 * i + 1] + s[:, 2 * i + 1 : 2 * i + 2]
+            return s[:, 3 * i : 3 * i + 1] + s[:, 3 * i + 1 : 3 * i + 2] + s[:, 3 * i + 2 : 3 * i + 3]
 
         for c in range(cross_heads):
             cols = slice(c * HD, (c + 1) * HD)
@@ -745,7 +747,7 @@
         and (weight.shape[1] // tensor) % WIDE == 0
         and aq.shape[0] % 16 == 0
         and vq.shape[0] % 16 == 0
-        and 4 * (cq.shape[1] // HD) <= HD
+        and 6 * (cq.shape[1] // HD) <= HD
         and (aq.size * seq) % (vq.shape[1] * 16) == 0
         and 2 * (seq + 1) * aq.size <= vq.size
         and weight.size * 2 <= 10 * 2**20

time: 37.7 us -> 37.7 us (level)
  no operation moved by 1% of the time
where the time goes in v6:
time: 37.7 us; the launch traced here: 37.6 us
  Pallas kernels  36.9 us (98%)
  between operations  0.64 us (2%)
    pallas_call x1, Pallas kernels, fused(): pl.pallas_call(functools.partial(block_kernel, seq, tensor), out_shape=tu...  36.2 us
    pallas_call x1, Pallas kernels, fused(): pl.pallas_call(write_out, out_shape=shapes, in_specs=[whole] * 3, out_spe...  0.78 us

profile of v6, /device:TPU:0, one launch (start us, length us, event | category | flops | bytes accessed | tf_op | source)
XLA Modules:
  0.0 37.6 jit_solution(561305335590154356)
XLA Ops:
  0.6 36.2 %shard_map.130 = (bf16[128,1024]{1,0:T(8,128)(2,1)S(1)}, bf16[128,512]{1,0:T(8,128)(2,1)S(1)}, bf16[16,512]{1,0:T(8,128)(2,1)S(1)}) custom-call(bf16[128,1024]{1,0:T(8,128)(2,1)} %vq.1, bf16[128,1024]{1,0:T(8,128)(2,1)} %vk.1, bf16[128,1024]{1,0:T(8,128)(2,1)} %vv.1, bf16[128,1024]{1,0:T(8,128)(2,1)} %vs.1, bf16[1024,4096]{1,0:T(8,128)(2,1)} %weight.1, ...), custom_call_target="tpu_custom_call" | custom-call | tf_op jit(solution)/shard_map/pallas_call | solution.py:680
  36.8 0.8 %shard_map.131 = (bf16[128,1024]{1,0:T(8,128)(2,1)}, bf16[128,512]{1,0:T(8,128)(2,1)}, bf16[16,512]{1,0:T(8,128)(2,1)}) custom-call(bf16[128,1024]{1,0:T(8,128)(2,1)S(1)} %get-tuple-element.6.refs_0_, bf16[128,512]{1,0:T(8,128)(2,1)S(1)} %get-tuple-element.7.refs_1_, bf16[16,512]{1,0:T(8,128)(2,1)S(1)} %get-tuple-element.8.refs_2_), custom_call_target="tpu_custom_call" | custom-call | tf_op jit(solution)/shard_map/pallas_call | solution.py:731

commit v7 on v6

--- a/solution.py
+++ b/solution.py
@@ -391,8 +391,8 @@
     run("tk1", first_tokens)
     run("tok", tokens)
     run("sib", meet)
+    run("K2", keys_to, peers[2])
     run("K1", keys_to, peers[1])
-    run("K2", keys_to, peers[2])
     run("q0", send_queries, 0)
     run("PE", early_part)
     run("p1", pass_audio, 1, 1)

time: 37.7 us -> 37.7 us (level)
  no operation moved by 1% of the time
where the time goes in v7:
time: 37.7 us; the launch traced here: 37.5 us
  Pallas kernels  36.9 us (98%)
  between operations  0.64 us (2%)
    pallas_call x1, Pallas kernels, fused(): pl.pallas_call(functools.partial(block_kernel, seq, tensor), out_shape=tu...  36.1 us
    pallas_call x1, Pallas kernels, fused(): pl.pallas_call(write_out, out_shape=shapes, in_specs=[whole] * 3, out_spe...  0.78 us

profile of v7, /device:TPU:0, one launch (start us, length us, event | category | flops | bytes accessed | tf_op | source)
XLA Modules:
  0.0 37.5 jit_solution(9300109223649698673)
XLA Ops:
  0.6 36.1 %shard_map.130 = (bf16[128,1024]{1,0:T(8,128)(2,1)S(1)}, bf16[128,512]{1,0:T(8,128)(2,1)S(1)}, bf16[16,512]{1,0:T(8,128)(2,1)S(1)}) custom-call(bf16[128,1024]{1,0:T(8,128)(2,1)} %vq.1, bf16[128,1024]{1,0:T(8,128)(2,1)} %vk.1, bf16[128,1024]{1,0:T(8,128)(2,1)} %vv.1, bf16[128,1024]{1,0:T(8,128)(2,1)} %vs.1, bf16[1024,4096]{1,0:T(8,128)(2,1)} %weight.1, ...), custom_call_target="tpu_custom_call" | custom-call | tf_op jit(solution)/shard_map/pallas_call | solution.py:680
  36.8 0.8 %shard_map.131 = (bf16[128,1024]{1,0:T(8,128)(2,1)}, bf16[128,512]{1,0:T(8,128)(2,1)}, bf16[16,512]{1,0:T(8,128)(2,1)}) custom-call(bf16[128,1024]{1,0:T(8,128)(2,1)S(1)} %get-tuple-element.6.refs_0_, bf16[128,512]{1,0:T(8,128)(2,1)S(1)} %get-tuple-element.7.refs_1_, bf16[16,512]{1,0:T(8,128)(2,1)S(1)} %get-tuple-element.8.refs_2_), custom_call_target="tpu_custom_call" | custom-call | tf_op jit(solution)/shard_map/pallas_call | solution.py:731
